TPU v7x, 32 devices: a whole 2x2x4 slice. The times are simulated.
32 devices in a mesh: groups: 1, dp: 32 (over z, y, x, core).
Axes of the slice: x: 2, y: 2, z: 4, core: 2. Of those that a mesh axis runs over, the one named last changes fastest.
Arguments:
- activations: bfloat16 [128, 8192], P(('groups', 'dp')), may hold values from -6 to 6
- cotangent: bfloat16 [128, 8192], P(('groups', 'dp')), may hold values from -6 to 6
- w_gate: bfloat16 [28672, 8192], P('dp'), may hold values from -0.0625 to 0.0625
- w_up: bfloat16 [28672, 8192], P('dp'), may hold values from -0.0625 to 0.0625
- w_down: bfloat16 [28672, 8192], P('dp'), may hold values from -0.03125 to 0.03125
- proj_model: bfloat16 [8192, 192], P('dp'), may hold values from -0.0625 to 0.0625
- proj_hidden: bfloat16 [28672, 192], P('dp'), may hold values from -0.03125 to 0.03125
- seq_ids: int32 [128], P('groups'), may hold values from 0 to 15, never falling along the last dimension, each value on 1 to 16 neighbouring positions
- targets: bfloat16 [256, 3, 64, 64], P(('groups', 'dp')), may hold values from -24 to 24
- target_domain: int32 [256], P(('groups', 'dp')), may hold values from 0 to 31, never falling along the last dimension, each value on 1 to 16 neighbouring positions
Outputs:
- sketches: float32 [16, 3, 64, 64], P('groups')
- scores: float32 [16, 32], P('groups')
Inputs may be any that keep to these rules, and one draw needn't show every extreme that they name: `seq_ids`: never falling along the tokens; each of the 16 sequences has 1 to 16 tokens, one exactly 16. `target_domain`: never falling along the target examples; each of the 32 domains has 1 to 16 examples, one exactly 16.
All inputs are finite; a program needn't handle non-finite values.
Results may differ from a plain program's by a relative error of at most 0.0032.
Values may be sent and summed in bfloat16 or wider, within the bound.
A program may use at most 128 MiB of HBM per device.

v0:
```python
import jax
import jax.numpy as jnp
from jax import lax
from jax.sharding import PartitionSpec as P

DOMAINS = 32
SEQS = 16


def sequence_sketch(vectors, onehot, rank_size):
    blocks = vectors.reshape(vectors.shape[0], 6, rank_size)
    left_side = jnp.stack((blocks[:, 4], blocks[:, 5], blocks[:, 3]), 1)
    right_side = jnp.stack((blocks[:, 0], blocks[:, 1], blocks[:, 2]), 1)
    return jnp.einsum(
        "ns,nka,nkb->skab", onehot, left_side, right_side, precision=lax.Precision.HIGHEST
    )


def on_device(
    activations,
    cotangent,
    w_gate,
    w_up,
    w_down,
    proj_model,
    proj_hidden,
    seq_ids,
    targets,
    target_domain,
):
    rank_size = proj_model.shape[1] // 3
    model_cols = proj_model.shape[0]
    hidden_units = w_gate.shape[0]
    position = lax.axis_index("dp")
    offset = position * model_cols
    rows_in = lax.all_gather(activations, "dp", axis=0, tiled=True)
    gate_value = jnp.einsum("rd,fd->rf", rows_in, w_gate, preferred_element_type=jnp.float32)
    up_value = jnp.einsum("rd,fd->rf", rows_in, w_up, preferred_element_type=jnp.float32)
    columns = lax.dynamic_slice_in_dim(rows_in, offset, model_cols, 1)
    in_model = jnp.dot(columns, proj_model[:, : 2 * rank_size], preferred_element_type=jnp.float32)
    gate_value, up_value, in_model = (gate_value, up_value, in_model)
    forward_all = jnp.concatenate([gate_value, up_value, in_model], 1)
    gate_all = forward_all[:, :hidden_units]
    up_all = forward_all[:, hidden_units : 2 * hidden_units]
    in_model_all = forward_all[:, 2 * hidden_units :]
    gate_value = gate_all
    up_value = up_all
    rows_grad = lax.all_gather(cotangent, "dp", axis=0, tiled=True)
    sigmoid_gate = jax.nn.sigmoid(gate_value)
    silu_gate = gate_value * sigmoid_gate
    hidden = (silu_gate * up_value).astype(jnp.bfloat16)
    grad_hidden = jnp.einsum("rd,fd->rf", rows_grad, w_down, preferred_element_type=jnp.float32)
    grad_gate = (
        grad_hidden * up_value * sigmoid_gate * (1.0 + gate_value * (1.0 - sigmoid_gate))
    ).astype(jnp.bfloat16)
    grad_up = (grad_hidden * silu_gate).astype(jnp.bfloat16)
    columns = lax.dynamic_slice_in_dim(rows_grad, offset, model_cols, 1)
    out_down = jnp.dot(columns, proj_model[:, 2 * rank_size :], preferred_element_type=jnp.float32)
    in_down = jnp.dot(hidden, proj_hidden[:, :rank_size], preferred_element_type=jnp.float32)
    out_gate = jnp.dot(
        grad_gate, proj_hidden[:, rank_size : 2 * rank_size], preferred_element_type=jnp.float32
    )
    out_up = jnp.dot(grad_up, proj_hidden[:, 2 * rank_size :], preferred_element_type=jnp.float32)
    grads_all = jnp.concatenate([out_down, in_down, out_gate, out_up], 1)
    partials = jnp.concatenate([in_model_all, grads_all], 1)
    sequence_range = jnp.arange(SEQS)
    own_vectors = lax.psum_scatter(partials, "dp", scatter_dimension=0, tiled=True)
    own_count = own_vectors.shape[0]
    own_ids = lax.dynamic_slice_in_dim(seq_ids, position * own_count, own_count, 0)
    own_onehot = (own_ids[:, None] == sequence_range[None, :]).astype(jnp.float32)
    local_sketch = sequence_sketch(own_vectors, own_onehot, rank_size)
    sketches = lax.psum(local_sketch, "dp")
    entries = 3 * rank_size * rank_size
    flat_sketch = sketches.reshape(SEQS, entries)
    inverse_norm = lax.rsqrt(jnp.sum(flat_sketch * flat_sketch, 1) + 1e-06)
    domain_onehot = (target_domain[None, :] == jnp.arange(DOMAINS)[:, None]).astype(jnp.bfloat16)
    local_targets = targets.reshape(targets.shape[0], entries)
    domain_count = jnp.sum(domain_onehot.astype(jnp.float32), 1)
    target_products = jnp.dot(
        flat_sketch, local_targets.astype(jnp.float32).T, precision=lax.Precision.HIGHEST
    )
    folded = jnp.dot(
        target_products, domain_onehot.astype(jnp.float32).T, precision=lax.Precision.HIGHEST
    )
    total_scores, total_count = lax.psum((folded, domain_count), "dp")
    scores = total_scores / total_count[None, :] * inverse_norm[:, None]
    return (sketches, scores)


def solution(mesh):
    in_specs = (
        P(("groups", "dp"), None),
        P(("groups", "dp"), None),
        P("dp", None),
        P("dp", None),
        P("dp", None),
        P("dp", None),
        P("dp", None),
        P("groups"),
        P(("groups", "dp"), None, None, None),
        P(("groups", "dp")),
    )
    out_specs = (P("groups", None, None, None), P("groups", None))
    return jax.shard_map(
        on_device, mesh=mesh, in_specs=in_specs, out_specs=out_specs, check_vma=False
    )
```

profile of v0, /device:TPU:0, one launch (start us, length us, event | category | flops | bytes accessed | tf_op | source)
XLA Modules:
  0.0 479.7 jit_solution(16426818172373653184)
XLA Ops:
  7.2 0.0 copy-start
  7.2 0.0 all-gather.5.cloned.1.call-start
  7.2 0.7 all-gather.5.cloned.1.call-update
  7.9 0.0 all-gather.7.cloned.1.call-start
  8.0 0.7 all-gather.7.cloned.1.call-update
  8.7 0.0 all-reduce.7.cloned.1.call-start
  8.7 0.7 dynamic_slice.11
  9.4 0.0 copy-start.3
  9.4 60.4 %all-gather.5.cloned.1.call-done = bf16[32,4,8192]{2,1,0:T(4,128)(2,1)} async-done(((bf16[1,4,8192]{2,1,0:T(4,128)(2,1)}), bf16[32,4,8192]{2,1,0:T(4,128)(2,1)}) %all-gather.5.cloned.1.call-update) | async-done | bytes 2097168 | tf_op jit(solution)/shard_map/all_gather | solution.py:36
  69.8 2.5 reshape.18
  72.3 0.0 copy-done.3
  72.4 0.1 convolution_dynamic-update-slice_fusion
  72.5 55.3 %all-gather.7.cloned.1.call-done = bf16[32,4,8192]{2,1,0:T(4,128)(2,1)} async-done(((bf16[1,4,8192]{2,1,0:T(4,128)(2,1)}), bf16[32,4,8192]{2,1,0:T(4,128)(2,1)}) %all-gather.7.cloned.1.call-update) | async-done | bytes 2097168 | tf_op jit(solution)/shard_map/all_gather | solution.py:48
  127.7 3.9 reshape.20
  131.7 1.0 convolution_dynamic-update-slice_fusion.4
  132.6 10.6 %fusion.30 = f32[128,896]{1,0:T(8,128)S(1)} fusion(bf16[128,8192]{1,0:T(8,128)(2,1)} %reshape.20, bf16[896,8192]{1,0:T(8,128)(2,1)} %param.14), kind=kOutput, calls=%fused_computation.45 | convolution fusion | flops 1879048192 | bytes 17235968 | tf_op jit(solution)/shard_map/rd,fd->rf/dot_general | solution.py:52
  143.2 9.9 %fusion.28 = f32[128,896]{1,0:T(8,128)S(1)} fusion(bf16[128,8192]{1,0:T(8,128)(2,1)S(1)} %reshape.18, bf16[896,8192]{1,0:T(8,128)(2,1)} %param.12), kind=kOutput, calls=%fused_computation.43 | convolution fusion | flops 1879048192 | bytes 17235968 | tf_op jit(solution)/shard_map/rd,fd->rf/dot_general | solution.py:37
  153.1 0.0 copy-start.4
  153.1 9.9 %fusion.29 = f32[128,896]{1,0:T(8,128)S(1)} fusion(bf16[128,8192]{1,0:T(8,128)(2,1)S(1)} %reshape.18, bf16[896,8192]{1,0:T(8,128)(2,1)} %param.13), kind=kOutput, calls=%fused_computation.44 | convolution fusion | flops 1879048192 | bytes 17235968 | tf_op jit(solution)/shard_map/rd,fd->rf/dot_general | solution.py:38
  163.1 0.0 copy-done.4
  163.1 0.3 convolution_dynamic-update-slice_fusion.3
  163.4 0.3 convolution_dynamic-update-slice_fusion.2
  163.7 0.3 convolution_dynamic-update-slice_fusion.1
  164.0 0.0 copy-start.2
  164.0 0.0 copy-start.5
  164.0 0.7 copy-done.2
  164.7 0.0 all-reduce.7.cloned.1.call-update
  164.7 0.2 all-reduce.5.cloned.1.call-start
  165.0 123.5 %all-reduce.7.cloned.1.call-done = f32[128,384]{0,1:T(8,128)} async-done(((f32[128,384]{0,1:T(8,128)}), f32[128,384]{0,1:T(8,128)}) %all-reduce.7.cloned.1.call-update) | async-done | bytes 196624
  288.4 1.0 constant_dynamic-slice_fusion
  289.5 0.1 copy.37
  289.6 0.1 copy.24
  289.7 3.9 convolution_bitcast_fusion
  293.5 0.0 all-reduce.5.cloned.1.call-update
  293.6 0.0 copy-done.5
  293.6 0.1 convert_reduce_fusion
  293.6 134.0 %all-reduce.5.cloned.1.call-done = f32[16,3,64,64]{3,2,0,1:T(8,128)} async-done(((f32[16,3,64,64]{3,2,0,1:T(8,128)}), f32[16,3,64,64]{3,2,0,1:T(8,128)}) %all-reduce.5.cloned.1.call-update) | async-done | bytes 786448 | tf_op jit(solution)/shard_map/psum | solution.py:72
  427.6 0.0 copy-start.1
  427.6 1.8 multiply_reduce_fusion
  429.4 0.0 copy-done
  429.4 0.1 copy-done.1
  429.5 2.3 fusion.2
  431.8 0.2 fusion.21
  432.0 39.2 %all-reduce.1 = (f32[16,32]{1,0:T(8,128)S(1)}, f32[32]{0:T(128)S(1)}) all-reduce(f32[16,32]{1,0:T(8,128)S(1)} %fusion.21, f32[32]{0:T(128)S(1)} %convert_reduce_fusion), channel_id=1, replica_groups=mesh['groups'=1,'dp'=32] {'dp'}, use_global_device_ids=true, to_apply=%region_2.0 | all-reduce | flops 544 | bytes 4352 | tf_op jit(solution)/shard_map/psum | solution.py:85
  471.3 0.7 divide_multiply_fusion
  471.9 1.2 copy.29
  (5 shorter events, 0.0 us)
Async XLA Ops:
  7.2 422.3 %copy-start = (bf16[8,3,64,64]{3,2,1,0:T(8,128)(2,1)S(1)}, bf16[8,3,64,64]{3,2,1,0:T(8,128)(2,1)}, u32[]{:S(2)}) copy-start(bf16[8,3,64,64]{3,2,1,0:T(8,128)(2,1)} %param.18) | copy-start | bytes 589828
  7.2 62.6 %all-gather.5.cloned.1.call-start = ((), (), s32[]{:S(2)}) async-start(), calls=%async_computation.1 | async-start | bytes 2162688 | tf_op jit(solution)/shard_map/all_gather | solution.py:36
  7.9 119.8 %all-gather.7.cloned.1.call-start = ((), (), s32[]{:S(2)}) async-start(), calls=%async_computation.2 | async-start | bytes 2162688 | tf_op jit(solution)/shard_map/all_gather | solution.py:48
  8.7 279.8 %all-reduce.7.cloned.1.call-start = ((), (), s32[]{:S(2)}) async-start(), calls=%async_computation.3 | async-start | bytes 393216
  9.4 62.9 %copy-start.3 = (bf16[256,192]{0,1:T(8,128)(2,1)S(1)}, bf16[256,192]{0,1:T(8,128)(2,1)}, u32[]{:S(2)}) copy-start(bf16[256,192]{0,1:T(8,128)(2,1)} %param.15) | copy-start | bytes 294916
  153.1 10.0 %copy-start.4 = (bf16[896,192]{0,1:T(8,128)(2,1)S(1)}, bf16[896,192]{0,1:T(8,128)(2,1)}, u32[]{:S(2)}) copy-start(bf16[896,192]{0,1:T(8,128)(2,1)} %param.16) | copy-start | bytes 1032196
  164.0 0.7 copy-start.2
  164.0 129.5 %copy-start.5 = (s32[8]{0:T(128)S(1)}, s32[8]{0:T(128)}, u32[]{:S(2)}) copy-start(s32[8]{0:T(128)} %param.19) | copy-start | bytes 100
  164.7 262.9 %all-reduce.5.cloned.1.call-start = ((), (), s32[]{:S(2)}) async-start(), calls=%async_computation | async-start | bytes 3145728 | tf_op jit(solution)/shard_map/psum | solution.py:72
  427.6 1.9 copy-start.1
Sparse Core Ops, SparseCore 0:
  10.8 58.9 all-gather.4
  72.7 55.0 all-gather.6
  164.8 123.5 all-reduce.6
  294.1 133.4 all-reduce.4
where the time goes:
time: 480 us
  waiting for transfers between devices  374 us (78%)
  blocking collectives  39.2 us (8%)
  matrix products  38.8 us (8%)
  between operations  13.9 us (3%)
  local copies, waits for them, and re-layouts  10.4 us (2%)
    psum x1, waiting for transfers between devices, on_device(): sketches = lax.psum(local_sketch, 'dp')  134 us
    unnamed x5, waiting for transfers between devices  125 us
    all_gather x1, waiting for transfers between devices, on_device(): rows_in = lax.all_gather(activations, 'dp', axis=0, tiled=True)  60.4 us
    all_gather x1, waiting for transfers between devices, on_device(): rows_grad = lax.all_gather(cotangent, 'dp', axis=0, tiled=True)  55.3 us
    psum x1, blocking collectives, on_device(): total_scores, total_count = lax.psum((folded, domain_count), 'dp')  39.2 us
    dot_general x1, matrix products, on_device(): jnp.einsum('rd,fd->rf', rows_grad, w_down, preferred_element_type=jnp.flo...  10.6 us
    dot_general x1, matrix products, on_device(): jnp.einsum('rd,fd->rf', rows_in, w_up, preferred_element_type=jnp.float32)  9.95 us
    dot_general x1, matrix products, on_device(): jnp.einsum('rd,fd->rf', rows_in, w_gate, preferred_element_type=jnp.float32)  9.9 us
  transfers between devices with their start and end apart: 4, of which 4 were waited for; matrix products, arithmetic and copies ran while one was open for 1% of the time, Pallas kernels for 0%

commit v1 on v0

v1 whole, which is shorter than its diff:
```python
import functools

import jax
import jax.numpy as jnp
from jax import lax
from jax.experimental import pallas as pl
from jax.experimental.pallas import tpu as pltpu
from jax.sharding import PartitionSpec as P

DOMAINS = 32
SEQS = 16
MESH = pl.DeviceIdType.MESH
ROUTES = 2
CHUNKS = 8


def routes_of(n):
    core = (2, 1)
    if n == 32:
        z, y, x = (4, 8), (2, 4), (2, 2)
        return ((z, y, x, core), (z, x, y, core))
    if n == 128:
        y, x = (8, 16), (8, 2)
        return ((y, x, core), (x, y, core))
    rest = (n // 2, 2)
    return ((rest, core), (rest, core))


def moved(index, size, stride, by):
    coord = lax.rem(lax.div(index, stride), size)
    return index + (lax.rem(coord + by, size) - coord) * stride


def kernel(
    n,
    act_ref, cot_ref, wg_ref, wu_ref, wd_ref, pm_ref, ph_ref, seq_ref, tgt_ref, dom_ref,
    sk_ref, score_ref,
    wbuf, xg, xs, gacc, uacc, dacc, part, rsbuf, red, vg, lm, prod, msg, msgbuf,
    w_sem, own_sem, ag_send, ag_recv, rs_send, rs_recv, bc_send, bc_recv, sc_send, sc_recv,
):
    me = lax.axis_index("dp")
    half = n // 2
    routes = routes_of(n)
    tokens, width = xs.shape[2], xs.shape[3]
    per_route = CHUNKS // ROUTES
    rank = pm_ref.shape[1] // 3
    hidden_units = wg_ref.shape[0]
    own_rows = act_ref.shape[1]

    def weight_copy(m, c):
        source = (wg_ref, wu_ref, wd_ref)[m]
        return pltpu.make_async_copy(
            source.at[:, pl.ds(c * width, width)], wbuf.at[m, c], w_sem.at[m, c]
        )

    own_copies = []
    for a, source in enumerate((act_ref, cot_ref)):
        for r in range(ROUTES):
            copy = pltpu.make_async_copy(source.at[r], xg.at[a, r, me], own_sem.at[a, r])
            copy.start()
            own_copies.append(copy)

    barrier = pltpu.get_barrier_semaphore()

    def greet(d, carry):
        pl.semaphore_signal(
            barrier, inc=1, device_id={"dp": lax.rem(me + d, n)}, device_id_type=MESH
        )
        return carry

    lax.fori_loop(1, n, greet, 0)
    for c in range(CHUNKS):
        weight_copy(0, c).start()
        weight_copy(1, c).start()
    for c in range(CHUNKS):
        weight_copy(2, c).start()
    for copy in own_copies:
        copy.wait()
    pl.semaphore_wait(barrier, n - 1)

    def held_before(r, stage):
        count = 1
        for size, _ in routes[r][:stage]:
            count = count * size
        return count

    def send_stage(a, r, stage):
        size, stride = routes[r][stage]
        done = routes[r][:stage]

        def step(i, carry):
            t, d = lax.div(i, size - 1), lax.rem(i, size - 1) + 1
            block = me
            for done_size, done_stride in done:
                block = moved(block, done_size, done_stride, done_size - lax.rem(t, done_size))
                t = lax.div(t, done_size)
            pltpu.make_async_remote_copy(
                src_ref=xg.at[a, r, block],
                dst_ref=xg.at[a, r, block],
                send_sem=ag_send.at[a, r],
                recv_sem=ag_recv.at[a, r, stage],
                device_id={"dp": moved(me, size, stride, d)},
                device_id_type=MESH,
            ).start()
            return carry

        lax.fori_loop(0, held_before(r, stage) * (size - 1), step, 0)

    def take_stage(a, r, stage):
        count = held_before(r, stage) * (routes[r][stage][0] - 1)
        blocks = xg.at[a, r, pl.ds(0, count)]
        pltpu.make_async_copy(blocks, blocks, ag_recv.at[a, r, stage]).wait()

    stages = len(routes[0])
    for a in range(2):
        for r in range(ROUTES):
            send_stage(a, r, 0)
    for stage in range(1, stages):
        for r in range(ROUTES):
            take_stage(0, r, stage - 1)
            send_stage(0, r, stage)

    def lay_out(a, r, q):
        c = r * per_route + q
        group = 16 // own_rows

        def step(g, carry):
            pieces = [
                xg[a, r, g * group + i, :, pl.ds(pl.multiple_of(q * width, width), width)].astype(jnp.float32)
                for i in range(group)
            ]
            xs[a, c, pl.ds(pl.multiple_of(g * 16, 16), 16), :] = jnp.concatenate(pieces, 0).astype(
                jnp.bfloat16
            )
            return carry

        lax.fori_loop(0, tokens // 16, step, 0)

    contract = (((1,), (1,)), ((), ()))

    def add_product(acc, a, m, c):
        acc[...] += lax.dot_general(
            xs[a, c], wbuf[m, c], contract, preferred_element_type=jnp.float32
        )

    gacc[...] = jnp.zeros_like(gacc)
    uacc[...] = jnp.zeros_like(uacc)
    dacc[...] = jnp.zeros_like(dacc)
    def relay(stage):
        if stage < stages:
            for r in range(ROUTES):
                take_stage(1, r, stage - 1)
                send_stage(1, r, stage)

    for r in range(ROUTES):
        take_stage(0, r, stages - 1)

        def gate_up(q, carry, r=r):
            c = r * per_route + q
            lay_out(0, r, q)
            weight_copy(0, c).wait()
            add_product(gacc, 0, 0, c)
            weight_copy(1, c).wait()
            add_product(uacc, 0, 1, c)
            return carry

        for part_of in range(2):
            relay(2 * r + part_of + 1)
            first = part_of * per_route // 2
            lax.fori_loop(first, first + per_route // 2, gate_up, 0)

    for r in range(ROUTES):
        take_stage(1, r, stages - 1)

        def down(q, carry, r=r):
            c = r * per_route + q
            lay_out(1, r, q)
            weight_copy(2, c).wait()
            add_product(dacc, 1, 2, c)
            return carry

        lax.fori_loop(0, per_route, down, 0)

    in_down = out_gate = out_up = jnp.zeros((tokens, rank), jnp.float32)
    for off in range(0, hidden_units, 256):
        cols = slice(off, min(off + 256, hidden_units))
        gate, up, grad = gacc[:, cols], uacc[:, cols], dacc[:, cols]
        sig = jax.nn.sigmoid(gate)
        silu = gate * sig
        hidden = (silu * up).astype(jnp.bfloat16)
        grad_gate = (grad * up * sig * (1.0 + gate * (1.0 - sig))).astype(jnp.bfloat16)
        grad_up = (grad * silu).astype(jnp.bfloat16)
        ph = ph_ref[cols, :]
        in_down += jnp.dot(hidden, ph[:, :rank], preferred_element_type=jnp.float32)
        out_gate += jnp.dot(grad_gate, ph[:, rank : 2 * rank], preferred_element_type=jnp.float32)
        out_up += jnp.dot(grad_up, ph[:, 2 * rank :], preferred_element_type=jnp.float32)

    window = pm_ref.shape[0]
    model_cols = CHUNKS * width // n
    start = lax.div(me * model_cols, window) * window
    own_chunk = lax.div(start, width)
    own_cols = pl.ds(pl.multiple_of(lax.rem(start, width), window), window)
    pm = pm_ref[...]
    rights = jnp.dot(xs[0, own_chunk, :, own_cols], pm[:, : 2 * rank], preferred_element_type=jnp.float32)
    out_down = jnp.dot(xs[1, own_chunk, :, own_cols], pm[:, 2 * rank :], preferred_element_type=jnp.float32)
    part[:, : 2 * rank] = jnp.concatenate([out_gate, out_up], 1)
    part[:, 2 * rank : 4 * rank] = jnp.concatenate([in_down, out_down], 1)
    part[:, 4 * rank :] = rights

    odd = lax.rem(me, 2)
    mine = lax.div(me, 2)

    def rows(j):
        return pl.ds(pl.multiple_of(j * 8, 8), 8)

    def to_reducer(d):
        j = lax.rem(mine + d, half)
        return pltpu.make_async_remote_copy(
            src_ref=part.at[rows(j)],
            dst_ref=rsbuf.at[me],
            send_sem=rs_send,
            recv_sem=rs_recv,
            device_id={"dp": 2 * j},
            device_id_type=MESH,
        )

    def scatter(d, carry):
        to_reducer(d).start()
        return carry

    lax.fori_loop(1, half, scatter, 0)

    @pl.when(odd == 1)
    def _():
        to_reducer(0).start()
        pltpu.make_async_copy(part, part, rs_send).wait()

    @pl.when(odd == 0)
    def _():
        pltpu.make_async_copy(part.at[rows(mine)], rsbuf.at[me], rs_recv).start()
        sent = part.at[pl.ds(0, 8 * (half - 1))]
        pltpu.make_async_copy(sent, sent, rs_send).wait()
        pltpu.make_async_copy(rsbuf, rsbuf, rs_recv).wait()
        red[...] = jnp.sum(rsbuf[...], 0)
        pltpu.make_async_copy(red, vg.at[rows(mine)], bc_recv).start()

        def share(d, carry):
            pltpu.make_async_remote_copy(
                src_ref=red,
                dst_ref=vg.at[rows(mine)],
                send_sem=bc_send,
                recv_sem=bc_recv,
                device_id={"dp": lax.rem(me + d, n)},
                device_id_type=MESH,
            ).start()
            return carry

        lax.fori_loop(1, n, share, 0)
        sent = rsbuf.at[pl.ds(0, n - 1)]
        pltpu.make_async_copy(sent, sent, bc_send).wait()

    for a in range(2):
        for r in range(ROUTES):
            count = 0
            for stage in range(stages):
                count += held_before(r, stage) * (routes[r][stage][0] - 1)
            sent = xg.at[a, r, pl.ds(0, count)]
            pltpu.make_async_copy(sent, sent, ag_send.at[a, r]).wait()

    pltpu.make_async_copy(vg, vg, bc_recv).wait()

    seq = seq_ref[...]
    outs = vg[:, : 2 * rank].T
    mixed = vg[:, 2 * rank : 4 * rank]
    ins = vg[:, 4 * rank :]
    lefts = (outs[:rank], outs[rank:], mixed.T[:rank])
    rights = (ins[:, :rank], ins[:, rank:], mixed[:, rank:])
    for k in range(3):
        left, right = lefts[k], rights[k]
        left_hi = left.astype(jnp.bfloat16).astype(jnp.float32)
        left_lo = left - left_hi
        for s in range(SEQS):
            here = seq == s
            hi = jnp.where(here, left_hi, 0.0).astype(jnp.bfloat16)
            lo = jnp.where(here, left_lo, 0.0).astype(jnp.bfloat16)
            block = slice(s * rank, (s + 1) * rank)
            lm[block, :tokens] = hi
            lm[block, tokens : 2 * tokens] = lo
            lm[block, 2 * tokens :] = hi
        right_hi = right.astype(jnp.bfloat16)
        right_lo = (right - right_hi.astype(jnp.float32)).astype(jnp.bfloat16)
        sketch = jnp.dot(
            lm[...], jnp.concatenate([right_hi, right_hi, right_lo], 0), preferred_element_type=jnp.float32
        )
        sk_ref[:, k] = sketch.reshape(SEQS, rank, rank)

    examples = tgt_ref.shape[0]

    def score(s, carry):
        squares = jnp.zeros((1, rank), jnp.float32)
        sums = [squares] * examples
        for k in range(3):
            block = sk_ref[s, k]
            squares = squares + jnp.sum(block * block, 0, keepdims=True)
            for e in range(examples):
                sums[e] = sums[e] + jnp.sum(block * tgt_ref[e, k].astype(jnp.float32), 0, keepdims=True)
        for e in range(examples):
            prod[e, pl.ds(s, 1), :] = sums[e]
        prod[examples, pl.ds(s, 1), :] = squares
        return carry

    lax.fori_loop(0, SEQS, score, 0)
    lane = lax.broadcasted_iota(jnp.int32, (SEQS, 128), 1)
    folded = jnp.zeros((SEQS, 128), jnp.float32)
    for e in range(examples):
        column = jnp.sum(prod[e], 1, keepdims=True)
        domain = dom_ref[e]
        folded += jnp.where(lane == domain, column, 0.0)
        folded += jnp.where(lane == domain + DOMAINS, 1.0, 0.0)
    inverse_norm = lax.rsqrt(jnp.sum(prod[examples], 1, keepdims=True) + 1e-06)
    msg[...] = folded
    pltpu.make_async_copy(msg, msgbuf.at[me], sc_recv).start()

    def spread(d, carry):
        pltpu.make_async_remote_copy(
            src_ref=msg,
            dst_ref=msgbuf.at[me],
            send_sem=sc_send,
            recv_sem=sc_recv,
            device_id={"dp": lax.rem(me + d, n)},
            device_id_type=MESH,
        ).start()
        return carry

    lax.fori_loop(1, n, spread, 0)
    sent = msgbuf.at[pl.ds(0, n - 1)]
    pltpu.make_async_copy(sent, sent, sc_send).wait()
    pltpu.make_async_copy(msgbuf, msgbuf, sc_recv).wait()
    total = jnp.sum(msgbuf[...], 0)
    score_ref[...] = total[:, :DOMAINS] / total[:, DOMAINS : 2 * DOMAINS] * inverse_norm


def on_device(n, activations, cotangent, w_gate, w_up, w_down, proj_model, proj_hidden, seq_ids, targets, target_domain):
    own_rows, model = activations.shape
    tokens = n * own_rows
    hidden_units = w_gate.shape[0]
    model_cols, features = proj_model.shape
    rank = features // 3
    width = model // CHUNKS
    stages = len(routes_of(n)[0])

    def by_route(x):
        return x.reshape(own_rows, ROUTES, model // ROUTES).transpose(1, 0, 2)

    if model_cols < 128:
        me = lax.axis_index("dp")
        padded = jnp.zeros((128, features), proj_model.dtype)
        proj_model = lax.dynamic_update_slice(padded, proj_model, ((me * model_cols) % 128, 0))
    vmem = pl.BlockSpec(memory_space=pltpu.VMEM)
    hbm = pl.BlockSpec(memory_space=pl.ANY)
    smem = pl.BlockSpec(memory_space=pltpu.SMEM)
    f32, bf16 = jnp.float32, jnp.bfloat16
    dma = pltpu.SemaphoreType.DMA
    return pl.pallas_call(
        functools.partial(kernel, n),
        out_shape=(
            jax.ShapeDtypeStruct((SEQS, 3, rank, rank), f32),
            jax.ShapeDtypeStruct((SEQS, DOMAINS), f32),
        ),
        in_specs=[vmem, vmem, hbm, hbm, hbm, vmem, vmem, vmem, vmem, smem],
        out_specs=(vmem, vmem),
        scratch_shapes=[
            pltpu.VMEM((3, CHUNKS, hidden_units, width), bf16),
            pltpu.VMEM((2, ROUTES, n, own_rows, model // ROUTES), bf16),
            pltpu.VMEM((2, CHUNKS, tokens, width), bf16),
            pltpu.VMEM((tokens, hidden_units), f32),
            pltpu.VMEM((tokens, hidden_units), f32),
            pltpu.VMEM((tokens, hidden_units), f32),
            pltpu.VMEM((tokens, 2 * features), f32),
            pltpu.VMEM((n, 8, 2 * features), f32),
            pltpu.VMEM((8, 2 * features), f32),
            pltpu.VMEM((tokens, 2 * features), f32),
            pltpu.VMEM((SEQS * rank, 3 * tokens), bf16),
            pltpu.VMEM((targets.shape[0] + 1, SEQS, rank), f32),
            pltpu.VMEM((SEQS, 128), f32),
            pltpu.VMEM((n, SEQS, 128), f32),
            dma((3, CHUNKS)),
            dma((2, ROUTES)),
            dma((2, ROUTES)),
            dma((2, ROUTES, stages)),
            dma(()),
            dma(()),
            dma(()),
            dma(()),
            dma(()),
            dma(()),
        ],
        compiler_params=pltpu.CompilerParams(
            collective_id=0, has_side_effects=True, vmem_limit_bytes=67000000
        ),
        name="sketch_scores",
    )(
        by_route(activations), by_route(cotangent), w_gate, w_up, w_down, proj_model, proj_hidden,
        seq_ids.reshape(1, tokens), targets, target_domain,
    )


def solution(mesh):
    in_specs = (
        P(("groups", "dp"), None),
        P(("groups", "dp"), None),
        P("dp", None),
        P("dp", None),
        P("dp", None),
        P("dp", None),
        P("dp", None),
        P("groups"),
        P(("groups", "dp"), None, None, None),
        P(("groups", "dp")),
    )
    out_specs = (P("groups", None, None, None), P("groups", None))
    return jax.shard_map(
        functools.partial(on_device, mesh.shape["dp"]),
        mesh=mesh, in_specs=in_specs, out_specs=out_specs, check_vma=False,
    )
```

time: 480 us -> 87.4 us (0.18)
  waiting for transfers between devices: 374 us -> 0 us
  Pallas kernels: 0 us -> 78.9 us
  blocking collectives: 39.2 us -> 0 us
  matrix products: 38.8 us -> 0 us
  between operations: 13.9 us -> 0.64 us
    psum x1 -> x0, waiting for transfers between devices: 134 us -> none  [on_device(): sketches = lax.psum(local_sketch, 'dp')]
    unnamed x5 -> x0, waiting for transfers between devices: 125 us -> none
    all_gather x2 -> x0, waiting for transfers between devices: 116 us -> none  [the longest x1 60.4 us: on_device(): rows_in = lax.all_gather(activations, 'dp', axis=0, tiled=True)]
    pallas_call x0 -> x1, Pallas kernels: none -> 78.9 us  [on_device(): pl.pallas_call(functools.partial(kernel, n), out_shape=(jax.ShapeDtypeStr...]
    psum x1 -> x0, blocking collectives: 39.2 us -> none  [on_device(): total_scores, total_count = lax.psum((folded, domain_count), 'dp')]
    dot_general x11 -> x0, matrix products: 38.8 us -> none  [the longest x1 10.6 us: on_device(): jnp.einsum('rd,fd->rf', rows_grad, w_down, preferred_element_type=jnp.flo...]
  transfers between devices with their start and end apart: 4 -> 0, of which waited for: 4 -> 0; matrix products, arithmetic and copies ran while one was open for 1% -> 0% of each run, Pallas kernels for 0% -> 0%
where the time goes in v1:
time: 87.4 us; the launch traced here: 87.1 us
  Pallas kernels  78.9 us (90%)
  local copies, waits for them, and re-layouts  7.62 us (9%)
    pallas_call x1, Pallas kernels, on_device(): pl.pallas_call(functools.partial(kernel, n), out_shape=(jax.ShapeDtypeStr...  78.9 us
    unnamed x4, local copies, waits for them, and re-layouts  7.62 us

profile of v1, /device:TPU:0, one launch (start us, length us, event | category | flops | bytes accessed | tf_op | source)
XLA Modules:
  0.0 87.1 jit_solution(11384768870838391819)
XLA Ops:
  0.6 1.6 %copy.12.pm_ref = bf16[256,192]{1,0:T(8,128)(2,1)} copy(bf16[256,192]{0,1:T(8,128)(2,1)} %param.15) | data formatting | bytes 196608 | tf_op args[5]
  2.3 2.0 %copy.13.ph_ref = bf16[896,192]{1,0:T(8,128)(2,1)} copy(bf16[896,192]{0,1:T(8,128)(2,1)} %param.16) | data formatting | bytes 688128 | tf_op args[6]
  4.2 78.9 %sketch_scores.1 = (f32[16,3,64,64]{3,2,1,0:T(8,128)}, f32[16,32]{1,0:T(8,128)}) custom-call(bf16[2,4,4096]{2,1,0:T(4,128)(2,1)} %bitcast.7, bf16[2,4,4096]{2,1,0:T(4,128)(2,1)} %bitcast.8, bf16[896,8192]{1,0:T(8,128)(2,1)} %wg_ref.1, bf16[896,8192]{1,0:T(8,128)(2,1)} %wu_ref.1, bf16[896,8192]{1,0:T(8,128)(2,1)} %wd_ref.1, bf16[256,192]{1,0:T(8,128)(2,1)} %copy.12.pm_ref, ...), custom_call_target="tpu_custom_call" | custom-call | tf_op jit(solution)/shard_map/sketch_scores/pallas_call | solution.py:364
  83.1 2.7 %copy.16 = f32[16,3,64,64]{3,2,1,0:T(8,128)} copy(f32[16,3,64,64]{3,2,1,0:T(8,128)} %get-tuple-element.4) | data formatting | bytes 1572864
  85.8 1.3 %copy.17 = f32[16,32]{1,0:T(8,128)} copy(f32[16,32]{1,0:T(8,128)} %get-tuple-element.5) | data formatting | bytes 4096

commit v2 on v1

--- a/solution.py
+++ b/solution.py
@@ -35,7 +35,7 @@
     n,
     act_ref, cot_ref, wg_ref, wu_ref, wd_ref, pm_ref, ph_ref, seq_ref, tgt_ref, dom_ref,
     sk_ref, score_ref,
-    wbuf, xg, xs, gacc, uacc, dacc, part, rsbuf, red, vg, lm, prod, msg, msgbuf,
+    wbuf, xg, xs, gacc, uacc, dacc, part, rsbuf, red, vg, lm, tf, prod, msg, msgbuf,
     w_sem, own_sem, ag_send, ag_recv, rs_send, rs_recv, bc_send, bc_recv, sc_send, sc_recv,
 ):
     me = lax.axis_index("dp")
@@ -115,6 +115,9 @@
     for a in range(2):
         for r in range(ROUTES):
             send_stage(a, r, 0)
+    examples = tgt_ref.shape[0]
+    for e in range(examples):
+        tf[e] = tgt_ref[e].astype(jnp.float32)
     for stage in range(1, stages):
         for r in range(ROUTES):
             take_stage(0, r, stage - 1)
@@ -134,7 +137,7 @@
             )
             return carry
 
-        lax.fori_loop(0, tokens // 16, step, 0)
+        lax.fori_loop(0, tokens // 16, step, 0, unroll=True)
 
     contract = (((1,), (1,)), ((), ()))
 
@@ -294,30 +297,36 @@
         )
         sk_ref[:, k] = sketch.reshape(SEQS, rank, rank)
 
-    examples = tgt_ref.shape[0]
-
     def score(s, carry):
-        squares = jnp.zeros((1, rank), jnp.float32)
+        squares = jnp.zeros((8, rank), jnp.float32)
         sums = [squares] * examples
         for k in range(3):
             block = sk_ref[s, k]
-            squares = squares + jnp.sum(block * block, 0, keepdims=True)
-            for e in range(examples):
-                sums[e] = sums[e] + jnp.sum(block * tgt_ref[e, k].astype(jnp.float32), 0, keepdims=True)
+            for i in range(0, rank, 8):
+                piece = block[i : i + 8]
+                squares = squares + piece * piece
+                for e in range(examples):
+                    sums[e] = sums[e] + piece * tf[e, k, i : i + 8, :]
         for e in range(examples):
-            prod[e, pl.ds(s, 1), :] = sums[e]
-        prod[examples, pl.ds(s, 1), :] = squares
+            prod[e, s] = sums[e]
+        prod[examples, s] = squares
         return carry
 
     lax.fori_loop(0, SEQS, score, 0)
-    lane = lax.broadcasted_iota(jnp.int32, (SEQS, 128), 1)
-    folded = jnp.zeros((SEQS, 128), jnp.float32)
+
+    def column_of(e):
+        return jnp.sum(jnp.sum(prod[e], 1), 1, keepdims=True)
+
+    top = SEQS // 2
+    lane = lax.broadcasted_iota(jnp.int32, (top, 128), 1)
+    folded = jnp.zeros((top, 128), jnp.float32)
     for e in range(examples):
-        column = jnp.sum(prod[e], 1, keepdims=True)
+        column = column_of(e)
         domain = dom_ref[e]
-        folded += jnp.where(lane == domain, column, 0.0)
-        folded += jnp.where(lane == domain + DOMAINS, 1.0, 0.0)
-    inverse_norm = lax.rsqrt(jnp.sum(prod[examples], 1, keepdims=True) + 1e-06)
+        folded += jnp.where(lane == domain, column[:top], 0.0)
+        folded += jnp.where(lane == domain + DOMAINS, column[top:], 0.0)
+        folded += jnp.where(lane == domain + 2 * DOMAINS, 1.0, 0.0)
+    inverse_norm = lax.rsqrt(column_of(examples) + 1e-06)
     msg[...] = folded
     pltpu.make_async_copy(msg, msgbuf.at[me], sc_recv).start()
 
@@ -337,7 +346,9 @@
     pltpu.make_async_copy(sent, sent, sc_send).wait()
     pltpu.make_async_copy(msgbuf, msgbuf, sc_recv).wait()
     total = jnp.sum(msgbuf[...], 0)
-    score_ref[...] = total[:, :DOMAINS] / total[:, DOMAINS : 2 * DOMAINS] * inverse_norm
+    counts = total[:, 2 * DOMAINS : 3 * DOMAINS]
+    score_ref[:top] = total[:, :DOMAINS] / counts * inverse_norm[:top]
+    score_ref[top:] = total[:, DOMAINS : 2 * DOMAINS] / counts * inverse_norm[top:]
 
 
 def on_device(n, activations, cotangent, w_gate, w_up, w_down, proj_model, proj_hidden, seq_ids, targets, target_domain):
@@ -381,9 +392,10 @@
             pltpu.VMEM((8, 2 * features), f32),
             pltpu.VMEM((tokens, 2 * features), f32),
             pltpu.VMEM((SEQS * rank, 3 * tokens), bf16),
-            pltpu.VMEM((targets.shape[0] + 1, SEQS, rank), f32),
-            pltpu.VMEM((SEQS, 128), f32),
-            pltpu.VMEM((n, SEQS, 128), f32),
+            pltpu.VMEM(targets.shape, f32),
+            pltpu.VMEM((targets.shape[0] + 1, SEQS, 8, rank), f32),
+            pltpu.VMEM((SEQS // 2, 128), f32),
+            pltpu.VMEM((n, SEQS // 2, 128), f32),
             dma((3, CHUNKS)),
             dma((2, ROUTES)),
             dma((2, ROUTES)),

time: 87.4 us -> 85.3 us (0.976)
  Pallas kernels: 78.9 us -> 76.7 us
    pallas_call x1, Pallas kernels: 78.9 us -> 76.7 us  [on_device(): pl.pallas_call(functools.partial(kernel, n), out_shape=(jax.ShapeDtypeStr...]
where the time goes in v2:
time: 85.3 us; the launch traced here: 85 us
  Pallas kernels  76.7 us (90%)
  local copies, waits for them, and re-layouts  7.62 us (9%)
    pallas_call x1, Pallas kernels, on_device(): pl.pallas_call(functools.partial(kernel, n), out_shape=(jax.ShapeDtypeStr...  76.7 us
    unnamed x4, local copies, waits for them, and re-layouts  7.62 us

profile of v2, /device:TPU:0, one launch (start us, length us, event | category | flops | bytes accessed | tf_op | source)
XLA Modules:
  0.0 85.0 jit_solution(3173846341869231439)
XLA Ops:
  0.6 1.6 %copy.12.pm_ref = bf16[256,192]{1,0:T(8,128)(2,1)} copy(bf16[256,192]{0,1:T(8,128)(2,1)} %param.15) | data formatting | bytes 196608 | tf_op args[5]
  2.3 2.0 %copy.13.ph_ref = bf16[896,192]{1,0:T(8,128)(2,1)} copy(bf16[896,192]{0,1:T(8,128)(2,1)} %param.16) | data formatting | bytes 688128 | tf_op args[6]
  4.2 76.7 %sketch_scores.1 = (f32[16,3,64,64]{3,2,1,0:T(8,128)}, f32[16,32]{1,0:T(8,128)}) custom-call(bf16[2,4,4096]{2,1,0:T(4,128)(2,1)} %bitcast.7, bf16[2,4,4096]{2,1,0:T(4,128)(2,1)} %bitcast.8, bf16[896,8192]{1,0:T(8,128)(2,1)} %wg_ref.1, bf16[896,8192]{1,0:T(8,128)(2,1)} %wu_ref.1, bf16[896,8192]{1,0:T(8,128)(2,1)} %wd_ref.1, bf16[256,192]{1,0:T(8,128)(2,1)} %copy.12.pm_ref, ...), custom_call_target="tpu_custom_call" | custom-call | tf_op jit(solution)/shard_map/sketch_scores/pallas_call | solution.py:375
  81.0 2.7 %copy.16 = f32[16,3,64,64]{3,2,1,0:T(8,128)} copy(f32[16,3,64,64]{3,2,1,0:T(8,128)} %get-tuple-element.4) | data formatting | bytes 1572864
  83.7 1.3 %copy.17 = f32[16,32]{1,0:T(8,128)} copy(f32[16,32]{1,0:T(8,128)} %get-tuple-element.5) | data formatting | bytes 4096
